TPU v7x, 512 devices: a whole 4x8x8 slice. The times are simulated.
512 devices in a mesh: seq: 64 (over z, y_hi, core), head: 8 (over x, y_lo).
Axes of the slice: x: 4, y: 8 (y_hi: 4, y_lo: 2; y = y_hi * 2 + y_lo), z: 8, core: 2. Of those that a mesh axis runs over, the one named last changes fastest.
Arguments:
- block_query_rows: bfloat16 [8192, 5120], P('seq', 'head'), may hold values from -180 to 180
- block_key_rows: bfloat16 [8192, 1024], P('seq', 'head'), may hold values from -6 to 6
- block_value_rows: bfloat16 [8192, 1024], P('seq', 'head'), may hold values from -6 to 6
- stretch_segments: int32 [8192], P('seq'), may hold values from 0 to 15, never falling along the last dimension, each value on 1 to 6144 neighbouring positions
- residual: bfloat16 [8192, 5120], P('seq', 'head'), may hold values from -6 to 6
- out_weight: bfloat16 [5120, 5120], P('head', 'seq'), may hold values from -0.25 to 0.25
- cache_by_prefill: bfloat16 [2, 2, 2048, 16, 1024], P(None, None, 'seq', None, 'head'), may hold values from -6 to 6
- request_pages: int32 [128], replicated, may hold values from 1 to 64, as said below
- request_owner: int32 [128], replicated, may hold values from 0 to 63, as said below
Outputs:
- layer_out: bfloat16 [8192, 5120], P('seq', 'head')
- cache_decode: bfloat16 [2, 2, 4096, 16, 1024], P(None, None, 'seq', None, 'head')
Inputs may be any that keep to these rules, and one draw needn't show every extreme that they name: `stretch_segments`: each request of the block holds at most 6144 tokens, and some request exactly that many. `request_pages`: the requests of one decode device hold at most 64 pages together, and those of some device exactly 64. `request_owner`: never falls along the requests; every device owns at least one request.
All inputs are finite; a program needn't handle non-finite values.
Results may differ from a plain program's by a relative error of at most 0.0065.
Values may be sent and summed in bfloat16 or wider, within the bound.
A program may use at most 128 MiB of HBM per device.

v0:
```python
import jax
import jax.numpy as jnp
from jax import lax
from jax.sharding import PartitionSpec as P

HEAD_SIZE = 128


def on_device(
    block_query_rows,
    block_key_rows,
    block_value_rows,
    stretch_segments,
    residual,
    out_weight,
    cache_by_prefill,
    request_pages,
    request_owner,
):
    seq_count = lax.axis_size("seq")
    seq_place = lax.axis_index("seq")
    rows = block_query_rows.shape[0]
    kv_local = block_key_rows.shape[1] // HEAD_SIZE
    query_groups = block_query_rows.shape[1] // block_key_rows.shape[1]
    query_four = block_query_rows.reshape(rows, kv_local, query_groups, HEAD_SIZE)
    query_place = seq_place * rows + jnp.arange(rows, dtype=jnp.int32)
    scale = HEAD_SIZE ** (-0.5)
    key_part = lax.all_gather(block_key_rows, "seq", axis=0, tiled=True)
    value_part = lax.all_gather(block_value_rows, "seq", axis=0, tiled=True)
    segment_part = lax.all_gather(stretch_segments, "seq", axis=0, tiled=True)
    count = key_part.shape[0]
    key_place = jnp.arange(count, dtype=jnp.int32)
    allowed = (
        (stretch_segments[:, None] == segment_part[None, :])
        & (query_place[:, None] >= key_place[None, :])
        & (key_place[None, :] >= 0)
    )
    running_max = jnp.full((kv_local, query_groups, rows), -1e30, jnp.float32)
    key_three = key_part.reshape(count, kv_local, HEAD_SIZE)
    value_three = value_part.reshape(count, kv_local, HEAD_SIZE)
    scores = (
        jnp.einsum("tkgd,pkd->kgtp", query_four, key_three, preferred_element_type=jnp.float32)
        * scale
    )
    masked = jnp.where(allowed, scores, -1e30)
    new_max = jnp.maximum(running_max, jnp.max(masked, axis=-1))
    weights = jnp.where(allowed, jnp.exp(masked - new_max[..., None]), 0.0)
    new_sum = jnp.sum(weights, axis=-1)
    contribution = jnp.einsum(
        "kgtp,pkd->kgtd",
        weights.astype(jnp.bfloat16),
        value_three,
        preferred_element_type=jnp.float32,
    )
    attention = (
        jnp.transpose(contribution / new_sum[..., None], (2, 0, 1, 3))
        .reshape(rows, -1)
        .astype(jnp.bfloat16)
    )
    partial_value = jnp.dot(
        attention,
        lax.all_gather(out_weight, "seq", axis=1, tiled=True),
        preferred_element_type=jnp.float32,
    )
    feature_width = partial_value.shape[1] // lax.axis_size("head")
    total = lax.psum(partial_value.astype(jnp.bfloat16), "head").astype(jnp.float32)
    mine = lax.dynamic_slice_in_dim(total, lax.axis_index("head") * feature_width, feature_width, 1)
    layer_out = (residual.astype(jnp.float32) + mine).astype(jnp.bfloat16)
    local_pages = cache_by_prefill.shape[2]
    capacity = 2 * local_pages
    per_pair = capacity // seq_count
    owners = jnp.arange(seq_count, dtype=jnp.int32)
    run_pages = jnp.sum(
        jnp.where(request_owner[None, :] == owners[:, None], request_pages[None, :], 0), axis=1
    )
    run_start = jnp.sum(
        jnp.where(request_owner[None, :] < owners[:, None], request_pages[None, :], 0), axis=1
    )
    pair_slots = jnp.arange(per_pair, dtype=jnp.int32)
    offset = (seq_place - run_start) % seq_count
    slot_index = pair_slots[None, :] * seq_count + offset[:, None]
    sending = slot_index < run_pages[:, None]
    local_index = pair_slots[None, :] + ((run_start + offset - seq_place) // seq_count)[:, None]
    local_index = jnp.where(sending, local_index, 0).reshape(-1)
    picked = jnp.take(cache_by_prefill, local_index, axis=2)
    outgoing = jnp.where(
        sending.reshape(-1)[None, None, :, None, None], picked, jnp.zeros_like(picked)
    )
    incoming = lax.all_to_all(outgoing, "seq", split_axis=2, concat_axis=2, tiled=True)
    layers, pair_kv, _, page_len, width = incoming.shape
    arranged = jnp.swapaxes(
        incoming.reshape(layers, pair_kv, seq_count, per_pair, page_len, width), 2, 3
    )
    my_start = run_start[seq_place]
    my_pages = run_pages[seq_place]
    rotated = jnp.roll(arranged, -my_start, axis=3).reshape(
        layers, pair_kv, capacity, page_len, width
    )
    keep = jnp.arange(capacity, dtype=jnp.int32) < my_pages
    cache_decode = jnp.where(keep[None, None, :, None, None], rotated, jnp.zeros_like(rotated))
    return (layer_out, cache_decode)


def solution(mesh):
    return jax.shard_map(
        on_device,
        mesh=mesh,
        in_specs=(
            P("seq", "head"),
            P("seq", "head"),
            P("seq", "head"),
            P("seq"),
            P("seq", "head"),
            P("head", "seq"),
            P(None, None, "seq", None, "head"),
            P(),
            P(),
        ),
        out_specs=(P("seq", "head"), P(None, None, "seq", None, "head")),
        check_vma=False,
    )
```

profile of v0, /device:TPU:16, one launch (start us, length us, event | category | flops | bytes accessed | tf_op | source)
XLA Modules:
  0.0 391.2 jit_solution(16656007094815539979)
XLA Ops:
  7.2 0.7 all-gather.5.cloned.1.call-update
  8.0 1.5 copy.27
  9.5 0.7 all-gather.9.cloned.1.call-update
  10.2 0.8 select_reduce_fusion.1
  11.0 0.8 gather_fusion
  11.9 1.2 select_bitcast_fusion
  13.1 16.5 %all-to-all-start = ((bf16[2,2,64,16,128]{4,3,1,0,2:T(8,128)(2,1)}), bf16[2,2,64,16,128]{4,3,1,0,2:T(8,128)(2,1)S(1)}, u32[]{:S(2)}, u32[]{:S(2)}) async-start(bf16[2,2,64,16,128]{4,3,1,0,2:T(8,128)(2,1)} %select_bitcast_fusion), calls=%async_computation | async-start | bytes 2097152 | tf_op jit(solution)/shard_map/all_to_all | solution.py:89
  29.5 0.0 all-reduce.2.cloned.1.call-start
  29.6 1.1 copy.25
  30.7 98.7 %all-gather = s32[64,1,128]{2,1,0:T(1,128)S(1)} all-gather(s32[1,1,128]{2,1,0:T(1,128)} %bitcast.79), channel_id=1, replica_groups=mesh['seq'=64,'head'=8] {'seq'}, dimensions={0}, use_global_device_ids=true | all-gather | bytes 33280 | tf_op jit(solution)/shard_map/all_gather | solution.py:30
  129.4 4.4 %fusion.7 = pred[128,8192]{0,1:T(8,128)(4,1)S(1)} fusion(s32[128]{0:T(128)S(1)} %iota_add_fusion, s32[128]{0:T(128)} %param.12, s32[8192]{0:T(1024)S(1)} %bitcast.78), kind=kLoop, calls=%fused_computation.11 | loop fusion | flops 3145728 | bytes 1082368 | tf_op jit(solution)/shard_map/and | solution.py:34
  133.8 4.7 %fusion = (f32[5,128]{1,0:T(8,128)S(1)}, f32[8192,128,5]{1,0,2:T(8,128)S(1)}) fusion(pred[128,8192]{0,1:T(8,128)(4,1)S(1)} %fusion.7, bf16[128,5,128]{0,2,1:T(8,128)(2,1)S(1)} %bitcast.76, bf16[8192,128]{1,0:T(8,128)(2,1)} %all-gather.5.cloned.1.call-done), kind=kOutput, calls=%fused_computation.3 | convolution fusion | flops 1357905280 | bytes 24283648 | tf_op jit(solution)/shard_map/tkgd,pkd->kgtp/dot_general | solution.py:42
  138.6 6.9 %copy-done.1 = f32[8192,128,5]{1,0,2:T(8,128)} copy-done((f32[8192,128,5]{1,0,2:T(8,128)}, f32[8192,128,5]{1,0,2:T(8,128)S(1)}, u32[]{:S(2)}) %copy-start.1) | copy-done | bytes 20971544
  145.5 5.2 %fusion.1 = f32[5,128]{1,0:T(8,128)S(1)} fusion(f32[8192,128,5]{1,0,2:T(8,128)S(1)} %get-tuple-element.7, f32[5,128]{1,0:T(8,128)S(1)} %broadcast_maximum_fusion, pred[128,8192]{0,1:T(8,128)(4,1)S(1)} %fusion.7), kind=kLoop, calls=%fused_computation.4 | loop fusion | flops 26213760 | bytes 22025216 | tf_op jit(solution)/shard_map/reduce_sum | solution.py:48
  150.7 40.7 %all-gather.7.cloned.1.call-done = bf16[8192,128]{0,1:T(8,128)(2,1)} async-done(((bf16[128,128]{0,1:T(8,128)(2,1)}), bf16[8192,128]{0,1:T(8,128)(2,1)}) %all-gather.7.cloned.1.call-update) | async-done | bytes 2097168 | tf_op jit(solution)/shard_map/all_gather | solution.py:29
  191.4 12.9 %fusion.16 = bf16[5,128,128]{1,2,0:T(8,128)(2,1)S(1)} fusion(f32[8192,128,5]{1,0,2:T(8,128)} %copy-done.1, f32[5,128]{1,0:T(8,128)S(1)} %broadcast_maximum_fusion, pred[128,8192]{0,1:T(8,128)(4,1)S(1)} %fusion.7, bf16[8192,128]{0,1:T(8,128)(2,1)} %all-gather.7.cloned.1.call-done, f32[5,128]{1,0:T(8,128)S(1)} %fusion.1), kind=kOutput, calls=%fused_computation.18 | convolution fusion | flops 1368555520 | bytes 24286208 | tf_op jit(solution)/shard_map/kgtp,pkd->kgtd/dot_general | solution.py:49
  204.4 81.0 %all-gather.9.cloned.1.call-done = bf16[640,5120]{0,1:T(8,128)(2,1)} async-done(((bf16[640,80]{0,1:T(8,128)(2,1)}), bf16[640,5120]{0,1:T(8,128)(2,1)}) %all-gather.9.cloned.1.call-update) | async-done | bytes 6553616 | tf_op jit(solution)/shard_map/all_gather | solution.py:62
  285.3 6.2 %convolution_convert_fusion = bf16[128,5120]{1,0:T(8,128)(2,1)} fusion(bf16[128,640]{0,1:T(8,128)(2,1)S(1)} %bitcast.77, bf16[640,5120]{0,1:T(8,128)(2,1)} %all-gather.9.cloned.1.call-done), kind=kOutput, calls=%fused_computation.9 | convolution fusion | flops 839516160 | bytes 8028160 | tf_op jit(solution)/shard_map/dot_general | solution.py:60
  291.5 0.6 dynamic_slice.14
  292.1 0.6 dynamic_slice.15
  294.1 0.7 iota_compare_fusion.3
  294.7 1.5 bitcast_select_fusion.1
  296.2 86.8 %all-reduce.2.cloned.1.call-done = bf16[128,5120]{1,0:T(8,128)(2,1)} async-done(((bf16[128,5120]{1,0:T(8,128)(2,1)}), bf16[128,5120]{1,0:T(8,128)(2,1)}) %all-reduce.2.cloned.1.call-update) | async-done | bytes 1310736 | tf_op jit(solution)/shard_map/psum | solution.py:66
  383.0 1.6 add_convert_fusion
  (17 shorter events, 0.3 us)
Async XLA Ops:
  7.2 3.9 copy-start
  7.2 126.6 %all-gather.5.cloned.1.call-start = ((), (), s32[]{:S(2)}) async-start(), calls=%async_computation.1 | async-start | bytes 2129920 | tf_op jit(solution)/shard_map/all_gather | solution.py:28
  7.9 183.5 %all-gather.7.cloned.1.call-start = ((), (), s32[]{:S(2)}) async-start(), calls=%async_computation.2 | async-start | bytes 2129920 | tf_op jit(solution)/shard_map/all_gather | solution.py:29
  9.5 275.9 %all-gather.9.cloned.1.call-start = ((), (), s32[]{:S(2)}) async-start(), calls=%async_computation.3 | async-start | bytes 6656000 | tf_op jit(solution)/shard_map/all_gather | solution.py:62
  13.1 281.6 %all-to-all-start = ((bf16[2,2,64,16,128]{4,3,1,0,2:T(8,128)(2,1)}), bf16[2,2,64,16,128]{4,3,1,0,2:T(8,128)(2,1)S(1)}, u32[]{:S(2)}, u32[]{:S(2)}) async-start(bf16[2,2,64,16,128]{4,3,1,0,2:T(8,128)(2,1)} %select_bitcast_fusion), calls=%async_computation | async-start | bytes 2097152 | tf_op jit(solution)/shard_map/all_to_all | solution.py:89
  29.5 353.5 %all-reduce.2.cloned.1.call-start = ((), (), s32[]{:S(2)}) async-start(), calls=%async_computation.4 | async-start | bytes 2621440 | tf_op jit(solution)/shard_map/psum | solution.py:66
  138.6 7.0 %copy-start.1 = (f32[8192,128,5]{1,0,2:T(8,128)}, f32[8192,128,5]{1,0,2:T(8,128)S(1)}, u32[]{:S(2)}) copy-start(f32[8192,128,5]{1,0,2:T(8,128)S(1)} %get-tuple-element.7) | copy-start | bytes 62914564
  204.3 178.7 %copy-start.2 = (bf16[128,640]{1,0:T(8,128)(2,1)S(1)}, bf16[128,640]{1,0:T(8,128)(2,1)}, u32[]{:S(2)}) copy-start(bf16[128,640]{1,0:T(8,128)(2,1)} %param.13) | copy-start | bytes 491524
Sparse Core Ops, SparseCore 0:
  11.3 100.3 all-gather.4
  115.5 75.8 all-gather.6
  194.7 90.5 all-gather.8
  291.6 91.3 all-reduce.1
where the time goes:
time: 392 us; the launch traced here: 391 us
  waiting for transfers between devices  210 us (54%)
  blocking collectives  98.7 us (25%)
  matrix products  23.8 us (6%)
  starting transfers between devices  16.6 us (4%)
  other arithmetic  15.4 us (4%)
  between operations  15.2 us (4%)
  local copies, waits for them, and re-layouts  11.5 us (3%)
    all_gather x1, blocking collectives, on_device(): segment_part = lax.all_gather(stretch_segments, 'seq', axis=0, tiled=True)  98.7 us
    psum x1, waiting for transfers between devices, on_device(): lax.psum(partial_value.astype(jnp.bfloat16), 'head').astype(jnp.float32)  86.8 us
    all_gather x1, waiting for transfers between devices, on_device(): lax.all_gather(out_weight, 'seq', axis=1, tiled=True)  81 us
    all_gather x1, waiting for transfers between devices, on_device(): value_part = lax.all_gather(block_value_rows, 'seq', axis=0, tiled=True)  40.7 us
    all_to_all x1, starting transfers between devices, on_device(): lax.all_to_all(outgoing, 'seq', split_axis=2, concat_axis=2, tiled=True)  16.5 us
    dot_general x1, matrix products, on_device(): jnp.einsum('kgtp,pkd->kgtd', weights.astype(jnp.bfloat16), value_three, p...  12.9 us
    unnamed x8, local copies, waits for them, and re-layouts  9.51 us
  transfers between devices with their start and end apart: 5, of which 3 were waited for; matrix products, arithmetic and copies ran while one was open for 11% of the time, Pallas kernels for 0%

commit v1 on v0

--- a/solution.py
+++ b/solution.py
@@ -63,7 +63,9 @@
         preferred_element_type=jnp.float32,
     )
     feature_width = partial_value.shape[1] // lax.axis_size("head")
-    total = lax.psum(partial_value.astype(jnp.bfloat16), "head").astype(jnp.float32)
+    total = jnp.sum(lax.all_gather(partial_value.astype(jnp.bfloat16), "head"), axis=0).astype(
+        jnp.float32
+    )
     mine = lax.dynamic_slice_in_dim(total, lax.axis_index("head") * feature_width, feature_width, 1)
     layer_out = (residual.astype(jnp.float32) + mine).astype(jnp.bfloat16)
     local_pages = cache_by_prefill.shape[2]

time: 392 us -> 528 us (1.35)
  the two profiles are of different devices: /device:TPU:16 before, /device:TPU:56 now
where the time goes in v1:
time: 528 us; the launch traced here: 527 us
  waiting for transfers between devices  367 us (70%)
  blocking collectives  81.5 us (15%)
  matrix products  23.8 us (5%)
  other arithmetic  19.6 us (4%)
  between operations  15.2 us (3%)
  local copies, waits for them, and re-layouts  11.6 us (2%)
  starting transfers between devices  8.63 us (2%)
    all_gather x1, waiting for transfers between devices, on_device(): lax.all_gather(partial_value.astype(jnp.bfloat16), 'head')  184 us
    all_gather x1, waiting for transfers between devices, on_device(): lax.all_gather(out_weight, 'seq', axis=1, tiled=True)  83.1 us
    all_gather x1, blocking collectives, on_device(): segment_part = lax.all_gather(stretch_segments, 'seq', axis=0, tiled=True)  81.5 us
    all_gather x1, waiting for transfers between devices, on_device(): value_part = lax.all_gather(block_value_rows, 'seq', axis=0, tiled=True)  61.9 us
    all_to_all x1, waiting for transfers between devices, on_device(): lax.all_to_all(outgoing, 'seq', split_axis=2, concat_axis=2, tiled=True)  34.4 us
    dot_general x1, matrix products, on_device(): jnp.einsum('kgtp,pkd->kgtd', weights.astype(jnp.bfloat16), value_three, p...  12.9 us
  transfers between devices with their start and end apart: 5, of which 5 were waited for; matrix products, arithmetic and copies ran while one was open for 7% of the time, Pallas kernels for 0%

profile of v1, /device:TPU:56, one launch (start us, length us, event | category | flops | bytes accessed | tf_op | source)
XLA Modules:
  0.0 527.2 jit_solution(7376060378971228269)
XLA Ops:
  7.2 0.7 all-gather.7.cloned.1.call-update
  8.0 1.5 copy.27
  9.5 0.7 all-gather.11.cloned.1.call-update
  10.2 1.1 copy.25
  11.3 81.5 %all-gather.1 = s32[64,1,128]{2,1,0:T(1,128)S(1)} all-gather(s32[1,1,128]{2,1,0:T(1,128)} %bitcast.81), channel_id=1, replica_groups=mesh['seq'=64,'head'=8] {'seq'}, dimensions={0}, use_global_device_ids=true | all-gather | bytes 33280 | tf_op jit(solution)/shard_map/all_gather | solution.py:30
  92.8 4.4 fusion.7
  97.2 1.9 all-gather.7.cloned.1.call-done
  99.2 4.7 fusion
  103.9 7.0 %copy-done.1 = f32[8192,128,5]{1,0,2:T(8,128)} copy-done((f32[8192,128,5]{1,0,2:T(8,128)}, f32[8192,128,5]{1,0,2:T(8,128)S(1)}, u32[]{:S(2)}) %copy-start.1) | copy-done | bytes 20971544
  110.9 5.2 fusion.1
  116.1 61.9 %all-gather.9.cloned.1.call-done = bf16[8192,128]{0,1:T(8,128)(2,1)} async-done(((bf16[128,128]{0,1:T(8,128)(2,1)}), bf16[8192,128]{0,1:T(8,128)(2,1)}) %all-gather.9.cloned.1.call-update) | async-done | bytes 2097168 | tf_op jit(solution)/shard_map/all_gather | solution.py:29
  178.0 12.9 %fusion.16 = bf16[5,128,128]{1,2,0:T(8,128)(2,1)S(1)} fusion(f32[8192,128,5]{1,0,2:T(8,128)} %copy-done.1, f32[5,128]{1,0:T(8,128)S(1)} %broadcast_maximum_fusion, pred[128,8192]{0,1:T(8,128)(4,1)S(1)} %fusion.7, bf16[8192,128]{0,1:T(8,128)(2,1)} %all-gather.9.cloned.1.call-done, f32[5,128]{1,0:T(8,128)S(1)} %fusion.1), kind=kOutput, calls=%fused_computation.18 | convolution fusion | flops 1368555520 | bytes 24286208 | tf_op jit(solution)/shard_map/kgtp,pkd->kgtd/dot_general | solution.py:49
  190.9 83.1 %all-gather.11.cloned.1.call-done = bf16[640,5120]{0,1:T(8,128)(2,1)} async-done(((bf16[640,80]{0,1:T(8,128)(2,1)}), bf16[640,5120]{0,1:T(8,128)(2,1)}) %all-gather.11.cloned.1.call-update) | async-done | bytes 6553616 | tf_op jit(solution)/shard_map/all_gather | solution.py:62
  274.0 6.2 %convolution_convert_fusion = bf16[128,5120]{1,0:T(8,128)(2,1)} fusion(bf16[128,640]{0,1:T(8,128)(2,1)S(1)} %bitcast.79, bf16[640,5120]{0,1:T(8,128)(2,1)} %all-gather.11.cloned.1.call-done), kind=kOutput, calls=%fused_computation.9 | convolution fusion | flops 839516160 | bytes 8028160 | tf_op jit(solution)/shard_map/dot_general | solution.py:60
  280.4 0.8 gather_fusion
  281.2 1.2 select_bitcast_fusion
  282.4 8.5 %all-to-all-start = ((bf16[2,2,64,16,128]{4,3,1,0,2:T(8,128)(2,1)}), bf16[2,2,64,16,128]{4,3,1,0,2:T(8,128)(2,1)S(1)}, u32[]{:S(2)}, u32[]{:S(2)}) async-start(bf16[2,2,64,16,128]{4,3,1,0,2:T(8,128)(2,1)} %select_bitcast_fusion), calls=%async_computation | async-start | bytes 2097152 | tf_op jit(solution)/shard_map/all_to_all | solution.py:91
  291.5 0.6 dynamic_slice.15
  293.4 0.7 iota_compare_fusion.3
  294.0 34.4 %all-to-all-done = bf16[2,2,64,16,128]{4,3,1,0,2:T(8,128)(2,1)S(1)} async-done(((bf16[2,2,64,16,128]{4,3,1,0,2:T(8,128)(2,1)}), bf16[2,2,64,16,128]{4,3,1,0,2:T(8,128)(2,1)S(1)}, u32[]{:S(2)}, u32[]{:S(2)}) %all-to-all-start) | async-done | bytes 1048608 | tf_op jit(solution)/shard_map/all_to_all | solution.py:91
  328.5 1.5 bitcast_select_fusion.1
  330.0 184.1 %all-gather.13.cloned.1.call-done = bf16[1024,5120]{1,0:T(8,128)(2,1)} async-done(((bf16[128,5120]{1,0:T(8,128)(2,1)}), bf16[1024,5120]{1,0:T(8,128)(2,1)}) %all-gather.13.cloned.1.call-update) | async-done | bytes 10485776 | tf_op jit(solution)/shard_map/all_gather | solution.py:66
  514.1 5.8 %reduce_sum.44 = bf16[128,5120]{1,0:T(8,128)(2,1)S(1)} reduce(bf16[8,128,5120]{2,1,0:T(8,128)(2,1)} %bitcast.76, bf16[]{:T(256)} %constant.79.clone.1), dimensions={0}, to_apply=%region_2.3 | reduce | flops 4587520 | bytes 11796482 | tf_op jit(solution)/shard_map/reduce_sum | solution.py:66
  520.0 0.7 add_convert_fusion
  (22 shorter events, 1.0 us)
Async XLA Ops:
  7.2 273.2 %copy-start = (bf16[2,2,32,16,128]{4,3,2,1,0:T(8,128)(2,1)S(1)}, bf16[2,2,32,16,128]{4,3,2,1,0:T(8,128)(2,1)}, u32[]{:S(2)}) copy-start(bf16[2,2,32,16,128]{4,3,2,1,0:T(8,128)(2,1)} %param.15) | copy-start | bytes 1572868
  7.2 92.0 %all-gather.7.cloned.1.call-start = ((), (), s32[]{:S(2)}) async-start(), calls=%async_computation.1 | async-start | bytes 2129920 | tf_op jit(solution)/shard_map/all_gather | solution.py:28
  7.9 170.0 %all-gather.9.cloned.1.call-start = ((), (), s32[]{:S(2)}) async-start(), calls=%async_computation.2 | async-start | bytes 2129920 | tf_op jit(solution)/shard_map/all_gather | solution.py:29
  9.5 264.5 %all-gather.11.cloned.1.call-start = ((), (), s32[]{:S(2)}) async-start(), calls=%async_computation.3 | async-start | bytes 6656000 | tf_op jit(solution)/shard_map/all_gather | solution.py:62
  10.2 503.9 %all-gather.13.cloned.1.call-start = ((), (), s32[]{:S(2)}) async-start(), calls=%async_computation.4 | async-start | bytes 11796480 | tf_op jit(solution)/shard_map/all_gather | solution.py:66
  103.9 7.0 %copy-start.1 = (f32[8192,128,5]{1,0,2:T(8,128)}, f32[8192,128,5]{1,0,2:T(8,128)S(1)}, u32[]{:S(2)}) copy-start(f32[8192,128,5]{1,0,2:T(8,128)S(1)} %get-tuple-element.7) | copy-start | bytes 62914564
  116.1 164.1 %copy-start.3 = (s32[128]{0:T(128)S(1)}, s32[128]{0:T(128)}, u32[]{:S(2)}) copy-start(s32[128]{0:T(128)} %param.16) | copy-start | bytes 1540
  116.1 164.1 %copy-start.4 = (s32[128]{0:T(128)S(1)}, s32[128]{0:T(128)}, u32[]{:S(2)}) copy-start(s32[128]{0:T(128)} %param.17) | copy-start | bytes 1540
  280.1 239.8 %copy-start.2 = (bf16[128,640]{1,0:T(8,128)(2,1)S(1)}, bf16[128,640]{1,0:T(8,128)(2,1)}, u32[]{:S(2)}) copy-start(bf16[128,640]{1,0:T(8,128)(2,1)} %param.13) | copy-start | bytes 491524
  282.4 46.1 %all-to-all-start = ((bf16[2,2,64,16,128]{4,3,1,0,2:T(8,128)(2,1)}), bf16[2,2,64,16,128]{4,3,1,0,2:T(8,128)(2,1)S(1)}, u32[]{:S(2)}, u32[]{:S(2)}) async-start(bf16[2,2,64,16,128]{4,3,1,0,2:T(8,128)(2,1)} %select_bitcast_fusion), calls=%async_computation | async-start | bytes 2097152 | tf_op jit(solution)/shard_map/all_to_all | solution.py:91
Sparse Core Ops, SparseCore 0:
  11.3 87.7 all-gather.6
  103.0 74.9 all-gather.8
  181.2 92.6 all-gather.10
  280.3 233.7 all-gather.12
